TPU v7x, 1024 devices: a whole 4x4x32 slice. The times are simulated.
1024 devices in a mesh: section: 128 (over z_lo, x, core), tensor: 8 (over z_hi, y).
Axes of the slice: x: 4, y: 4, z: 32 (z_hi: 2, z_lo: 16; z = z_hi * 16 + z_lo), core: 2. Of those that a mesh axis runs over, the one named last changes fastest.
Arguments:
- x_sent: bfloat16 [128, 128, 8192], P('section', None, 'tensor'), may hold values from -6 to 6
- grad_in: bfloat16 [128, 128, 8192], P('section', None, 'tensor'), may hold values from -4 to 4
- norm_gain: float32 [128, 8192], P('section', 'tensor'), may hold values from 0.25 to 1.75
- w_key: bfloat16 [128, 8192, 1024], P('section', 'tensor'), may hold values from -0.0625 to 0.0625
- key_grad: bfloat16 [128, 128, 1024], P('section'), may hold values from -6 to 6
- held_in: bfloat16 [128, 128, 8192], P('section', None, 'tensor'), may hold values from -1 to 1
- held_scale: float32 [128, 128, 64], P('section', None, 'tensor'), may hold values from 0.25 to 4
- stash_flags: int32 [128, 2], replicated, may hold values from 0 to 1, as said below
Outputs:
- key_rows: bfloat16 [128, 128, 1024], P('section', 'tensor')
- held_out: bfloat16 [128, 128, 8192], P('section', None, 'tensor')
- scale_out: float32 [128, 128, 64], P('section', None, 'tensor')
- grad_out: bfloat16 [128, 128, 8192], P('section', None, 'tensor')
Inputs may be any that keep to these rules, and one draw needn't show every extreme that they name: stash_flags[s, c] == stash_flags[127 - s, c]; in each column some mirror pair has flag 1 and some has flag 0.
All inputs are finite; a program needn't handle non-finite values. Where the computation divides by a largest or mean magnitude, that divisor is 1e-20 or more.
Results may differ from a plain program's by a relative error of at most 0.013.
Values may be sent and summed in bfloat16 or wider, within the bound.
A program may use at most 32 MiB of HBM per device.

v0:
```python
import jax
import jax.numpy as jnp
from jax import lax
from jax.sharding import PartitionSpec as P

D = 8192
BLOCK = 128


epsilon_norm = 1e-05
epsilon_scale = 1e-06


def shifted(block, axis, distance):
    devices = range(lax.axis_size(axis))
    route = [((i - distance) % len(devices), i) for i in devices]
    return lax.ppermute(block, axis, route)


def swapped(block, axis, apart):
    count = lax.axis_size(axis)
    route = []
    for low in range(count):
        high = low | 1 << apart
        if high != low and high < count:
            route += [(low, high), (high, low)]
    return lax.ppermute(block, axis, route)


def quantize(values):
    row_count = values.shape[0]
    blocks = values.reshape(row_count, -1, BLOCK)
    block_scale = jnp.max(jnp.abs(blocks), axis=-1) + epsilon_scale
    packed = (blocks / block_scale[..., None]).astype(jnp.bfloat16)
    return (packed.reshape(row_count, -1), block_scale)


def restore(packed, block_scale):
    row_count = packed.shape[0]
    blocks = packed.astype(jnp.float32).reshape(row_count, -1, BLOCK)
    return (blocks * block_scale[..., None]).reshape(row_count, -1)


def bit_list(bit_count):
    return list(range(bit_count))


def on_device(x_sent, grad_in, norm_gain, w_key, key_grad, held_in, held_scale, stash_flags):
    bit_count = lax.axis_size("section").bit_length() - 1
    position = lax.axis_index("section")
    own_flags = lax.dynamic_index_in_dim(stash_flags, position, 0, keepdims=False)
    fetched = own_flags[0] == 1
    parked = own_flags[1] == 1
    weight = w_key[0]
    gain_row = norm_gain[0]
    arrived = shifted(x_sent, "section", 1)[0]
    downward = shifted(grad_in, "section", -1)[0]
    stash_q = held_in[0]
    stash_s = held_scale[0]
    for bit in bit_list(bit_count):
        stash_q, stash_s = (
            swapped(stash_q, "section", bit),
            swapped(stash_s.astype(jnp.bfloat16), "section", bit).astype(stash_s.dtype),
        )
    forward_in = arrived.astype(jnp.float32)
    new_stash, new_scale = quantize(forward_in)
    out_q = new_stash
    out_s = new_scale
    for bit in bit_list(bit_count):
        out_q, out_s = (
            swapped(out_q, "section", bit),
            swapped(out_s.astype(jnp.bfloat16), "section", bit).astype(out_s.dtype),
        )
    source_q = jnp.where(fetched, stash_q, held_in[0])
    source_s = jnp.where(fetched, stash_s, held_scale[0])
    saved = restore(source_q, source_s)
    dnormed = lax.dot_general(
        key_grad[0], weight, (((1,), (1,)), ((), ())), preferred_element_type=jnp.float32
    )
    scaled = gain_row * dnormed
    forward_local = jnp.sum(forward_in * forward_in, axis=-1)
    saved_local = jnp.sum(saved * saved, axis=-1)
    cross_local = jnp.sum(saved * scaled, axis=-1)
    forward_total = lax.psum(forward_local, "tensor")
    saved_total, cross_total = lax.psum((saved_local, cross_local), "tensor")
    forward_inverse = lax.rsqrt(forward_total / D + epsilon_norm)[:, None]
    normed = (forward_in * forward_inverse * gain_row).astype(jnp.bfloat16)
    key_rows = lax.psum_scatter(
        jnp.dot(normed, weight, preferred_element_type=jnp.float32).astype(jnp.bfloat16),
        "tensor",
        scatter_dimension=0,
        tiled=True,
    )
    inverse = lax.rsqrt(saved_total / D + epsilon_norm)[:, None]
    cross_mean = (cross_total / D)[:, None]
    input_grad = inverse * scaled - saved * inverse**3 * cross_mean
    grad_out = (downward.astype(jnp.float32) + input_grad).astype(jnp.bfloat16)
    held_out = jnp.where(parked, out_q, new_stash)
    scale_out = jnp.where(parked, out_s, new_scale)
    return (key_rows[None], held_out[None], scale_out[None], grad_out[None])


def solution(mesh):
    return jax.shard_map(
        on_device,
        mesh=mesh,
        in_specs=(
            P("section", None, "tensor"),
            P("section", None, "tensor"),
            P("section", "tensor"),
            P("section", "tensor", None),
            P("section", None, None),
            P("section", None, "tensor"),
            P("section", None, "tensor"),
            P(),
        ),
        out_specs=(
            P("section", "tensor", None),
            P("section", None, "tensor"),
            P("section", None, "tensor"),
            P("section", None, "tensor"),
        ),
        check_vma=False,
    )
```

profile of v0, /device:TPU:2, one launch (start us, length us, event | category | flops | bytes accessed | tf_op | source)
XLA Modules:
  0.0 482.6 jit_solution(8060025177791328926)
XLA Ops:
  18.8 33.5 %collective-permute-start.9 = (bf16[128,8]{1,0:T(8,128)(2,1)S(1)}, bf16[128,8]{1,0:T(8,128)(2,1)S(1)}, u32[]{:S(2)}, u32[]{:S(2)}) collective-permute-start(bf16[128,8]{1,0:T(8,128)(2,1)S(1)} %collective-permute-done.8), channel_id=1, source_target_pairs={{0,16},{16,0},{8,24},{24,8},{32,48},{48,32},{40,56},{56,40},{64,80... | collective-permute-start | bytes 6152 | tf_op jit(solution)/shard_map/ppermute | solution.py:27
  56.0 5.4 %collective-permute-done.10 = bf16[128,8]{1,0:T(8,128)(2,1)S(1)} collective-permute-done((bf16[128,8]{1,0:T(8,128)(2,1)S(1)}, bf16[128,8]{1,0:T(8,128)(2,1)S(1)}, u32[]{:S(2)}, u32[]{:S(2)}) %collective-permute-start.10) | collective-permute-done | bytes 2080 | tf_op jit(solution)/shard_map/ppermute | solution.py:27
  63.3 3.9 collective-permute-done.11
  69.2 4.8 collective-permute-done.12
  75.9 7.9 %collective-permute-done.13 = bf16[128,8]{1,0:T(8,128)(2,1)S(1)} collective-permute-done((bf16[128,8]{1,0:T(8,128)(2,1)S(1)}, bf16[128,8]{1,0:T(8,128)(2,1)S(1)}, u32[]{:S(2)}, u32[]{:S(2)}) %collective-permute-start.13) | collective-permute-done | bytes 2080 | tf_op jit(solution)/shard_map/ppermute | solution.py:27
  86.9 3.9 collective-permute-start.17
  90.8 8.3 %collective-permute-done.14 = bf16[128,8]{1,0:T(8,128)(2,1)S(1)} collective-permute-done((bf16[128,8]{1,0:T(8,128)(2,1)S(1)}, bf16[128,8]{1,0:T(8,128)(2,1)S(1)}, u32[]{:S(2)}, u32[]{:S(2)}) %collective-permute-start.14) | collective-permute-done | bytes 2080 | tf_op jit(solution)/shard_map/ppermute | solution.py:27
  103.4 3.9 collective-permute-start.2
  107.4 6.7 %collective-permute-done.18 = bf16[128,1024]{1,0:T(8,128)(2,1)S(1)} collective-permute-done((bf16[128,1024]{1,0:T(8,128)(2,1)S(1)}, bf16[128,1024]{1,0:T(8,128)(2,1)S(1)}, u32[]{:S(2)}, u32[]{:S(2)}) %collective-permute-start.18) | collective-permute-done | bytes 262176 | tf_op jit(solution)/shard_map/ppermute | solution.py:27
  118.0 4.5 collective-permute-start.3
  125.3 4.3 collective-permute-done.3
  131.7 6.6 %collective-permute-done.20 = bf16[128,1024]{1,0:T(8,128)(2,1)S(1)} collective-permute-done((bf16[128,1024]{1,0:T(8,128)(2,1)S(1)}, bf16[128,1024]{1,0:T(8,128)(2,1)S(1)}, u32[]{:S(2)}, u32[]{:S(2)}) %collective-permute-start.20) | collective-permute-done | bytes 262176 | tf_op jit(solution)/shard_map/ppermute | solution.py:27
  151.9 3.9 collective-permute-done.25
  163.4 4.4 collective-permute-done.27
  167.8 7.6 %collective-permute-start.28 = (bf16[128,8]{0,1:T(8,128)(2,1)S(1)}, bf16[128,8]{0,1:T(8,128)(2,1)S(1)}, u32[]{:S(2)}, u32[]{:S(2)}) collective-permute-start(bf16[128,8]{0,1:T(8,128)(2,1)S(1)} %collective-permute-done.27), channel_id=1, source_target_pairs={{0,256},{256,0},{8,264},{264,8},{16,272},{272,16},{24,280},{280,24... | collective-permute-start | bytes 6152 | tf_op jit(solution)/shard_map/ppermute | solution.py:27
  177.4 4.8 %collective-permute-start.29 = (bf16[128,8]{0,1:T(8,128)(2,1)S(1)}, bf16[128,8]{0,1:T(8,128)(2,1)S(1)}, u32[]{:S(2)}, u32[]{:S(2)}) collective-permute-start(bf16[128,8]{0,1:T(8,128)(2,1)S(1)} %collective-permute-done.28), channel_id=1, source_target_pairs={{0,512},{512,0},{8,520},{520,8},{16,528},{528,16},{24,536},{536,24... | collective-permute-start | bytes 6152 | tf_op jit(solution)/shard_map/ppermute | solution.py:27
  182.3 4.8 collective-permute-start.5
  187.1 6.8 %collective-permute-start.22 = (bf16[128,1024]{1,0:T(8,128)(2,1)}, bf16[128,1024]{1,0:T(8,128)(2,1)S(1)}, u32[]{:S(2)}, u32[]{:S(2)}) collective-permute-start(bf16[128,1024]{1,0:T(8,128)(2,1)} %collective-permute-done.21), channel_id=1, source_target_pairs={{0,512},{512,0},{8,520},{520,8},{16,528},{528,16},{24,536},{536,24... | collective-permute-start | bytes 786440 | tf_op jit(solution)/shard_map/ppermute | solution.py:27
  199.8 3.9 collective-permute-start.6
  203.7 35.9 %collective-permute-done.22 = bf16[128,1024]{1,0:T(8,128)(2,1)S(1)} collective-permute-done((bf16[128,1024]{1,0:T(8,128)(2,1)}, bf16[128,1024]{1,0:T(8,128)(2,1)S(1)}, u32[]{:S(2)}, u32[]{:S(2)}) %collective-permute-start.22) | collective-permute-done | bytes 262176 | tf_op jit(solution)/shard_map/ppermute | solution.py:27
  241.5 69.4 %all-reduce = (f32[128]{0:T(128)S(1)}, f32[128]{0:T(128)S(1)}, f32[128]{0:T(128)S(1)}) all-reduce(f32[128]{0:T(128)S(1)} %get-tuple-element.15, f32[128]{0:T(128)S(1)} %get-tuple-element.9, f32[128]{0:T(128)S(1)} %get-tuple-element.8), channel_id=1, replica_groups=mesh['section'=128,'tensor'=8] {'tensor'}, use_global_device_ids=true, to_apply=%region_1.2 | all-reduce | flops 384 | bytes 3072 | tf_op jit(solution)/shard_map/psum | solution.py:84
  312.2 5.6 %collective-permute-start.7 = (bf16[128,1024]{1,0:T(8,128)(2,1)}, bf16[128,1024]{1,0:T(8,128)(2,1)S(1)}, u32[]{:S(2)}, u32[]{:S(2)}) collective-permute-start(bf16[128,1024]{1,0:T(8,128)(2,1)} %collective-permute-done.6), channel_id=1, source_target_pairs={{0,512},{512,0},{8,520},{520,8},{16,528},{528,16},{24,536},{536,24... | collective-permute-start | bytes 786440 | tf_op jit(solution)/shard_map/ppermute | solution.py:27
  319.6 44.1 %collective-permute-done.7 = bf16[128,1024]{1,0:T(8,128)(2,1)S(1)} collective-permute-done((bf16[128,1024]{1,0:T(8,128)(2,1)}, bf16[128,1024]{1,0:T(8,128)(2,1)S(1)}, u32[]{:S(2)}, u32[]{:S(2)}) %collective-permute-start.7) | collective-permute-done | bytes 262176 | tf_op jit(solution)/shard_map/ppermute | solution.py:27
  365.4 110.4 %reduce-scatter.2.cloned.1.call-done = bf16[16,1024]{1,0:T(8,128)(2,1)} async-done(((bf16[128,1024]{1,0:T(8,128)(2,1)}), bf16[16,1024]{1,0:T(8,128)(2,1)}) %reduce-scatter.2.cloned.1.call-update) | async-done | bytes 32784 | tf_op jit(solution)/shard_map/reduce_scatter | solution.py:88
  (76 shorter events, 71.4 us)
Async XLA Ops:
  7.2 468.6 %reduce-scatter.2.cloned.1.call-start = ((), (), s32[]{:S(2)}) async-start(), calls=%async_computation.1 | async-start | bytes 294912 | tf_op jit(solution)/shard_map/reduce_scatter | solution.py:88
  7.2 8.0 %collective-permute-start = (bf16[1,128,1024]{2,1,0:T(8,128)(2,1)}, bf16[1,128,1024]{2,1,0:T(8,128)(2,1)S(1)}, u32[]{:S(2)}, u32[]{:S(2)}) collective-permute-start(bf16[1,128,1024]{2,1,0:T(8,128)(2,1)} %param.8), channel_id=1, source_target_pairs={{1016,0},{0,8},{8,16},{16,24},{24,32},{32,40},{40,48},{48,56},{56,... | collective-permute-start | bytes 786440 | tf_op jit(solution)/shard_map/ppermute | solution.py:17
  9.3 77.5 %collective-permute-start.16 = (bf16[128,1024]{1,0:T(8,128)(2,1)}, bf16[128,1024]{1,0:T(8,128)(2,1)}, u32[]{:S(2)}, u32[]{:S(2)}) collective-permute-start(bf16[128,1024]{1,0:T(8,128)(2,1)} %bitcast.58), channel_id=1, source_target_pairs={{0,8},{8,0},{16,24},{24,16},{32,40},{40,32},{48,56},{56,48},{64,72... | collective-permute-start | bytes 786440 | tf_op jit(solution)/shard_map/ppermute | solution.py:27
  18.8 35.4 %collective-permute-start.9 = (bf16[128,8]{1,0:T(8,128)(2,1)S(1)}, bf16[128,8]{1,0:T(8,128)(2,1)S(1)}, u32[]{:S(2)}, u32[]{:S(2)}) collective-permute-start(bf16[128,8]{1,0:T(8,128)(2,1)S(1)} %collective-permute-done.8), channel_id=1, source_target_pairs={{0,16},{16,0},{8,24},{24,8},{32,48},{48,32},{40,56},{56,40},{64,80... | collective-permute-start | bytes 6152 | tf_op jit(solution)/shard_map/ppermute | solution.py:27
  54.1 7.3 %collective-permute-start.10 = (bf16[128,8]{1,0:T(8,128)(2,1)S(1)}, bf16[128,8]{1,0:T(8,128)(2,1)S(1)}, u32[]{:S(2)}, u32[]{:S(2)}) collective-permute-start(bf16[128,8]{1,0:T(8,128)(2,1)S(1)} %collective-permute-done.9), channel_id=1, source_target_pairs={{0,32},{32,0},{8,40},{40,8},{16,48},{48,16},{24,56},{56,24},{64,96... | collective-permute-start | bytes 6152 | tf_op jit(solution)/shard_map/ppermute | solution.py:27
  67.2 6.7 %collective-permute-start.12 = (bf16[128,8]{1,0:T(8,128)(2,1)S(1)}, bf16[128,8]{1,0:T(8,128)(2,1)S(1)}, u32[]{:S(2)}, u32[]{:S(2)}) collective-permute-start(bf16[128,8]{1,0:T(8,128)(2,1)S(1)} %collective-permute-done.11), channel_id=1, source_target_pairs={{0,128},{128,0},{8,136},{136,8},{16,144},{144,16},{24,152},{152,24... | collective-permute-start | bytes 6152 | tf_op jit(solution)/shard_map/ppermute | solution.py:27
  73.9 9.9 %collective-permute-start.13 = (bf16[128,8]{1,0:T(8,128)(2,1)S(1)}, bf16[128,8]{1,0:T(8,128)(2,1)S(1)}, u32[]{:S(2)}, u32[]{:S(2)}) collective-permute-start(bf16[128,8]{1,0:T(8,128)(2,1)S(1)} %collective-permute-done.12), channel_id=1, source_target_pairs={{0,256},{256,0},{8,264},{264,8},{16,272},{272,16},{24,280},{280,24... | collective-permute-start | bytes 6152 | tf_op jit(solution)/shard_map/ppermute | solution.py:27
  83.8 15.4 %collective-permute-start.14 = (bf16[128,8]{1,0:T(8,128)(2,1)S(1)}, bf16[128,8]{1,0:T(8,128)(2,1)S(1)}, u32[]{:S(2)}, u32[]{:S(2)}) collective-permute-start(bf16[128,8]{1,0:T(8,128)(2,1)S(1)} %collective-permute-done.13), channel_id=1, source_target_pairs={{0,512},{512,0},{8,520},{520,8},{16,528},{528,16},{24,536},{536,24... | collective-permute-start | bytes 6152 | tf_op jit(solution)/shard_map/ppermute | solution.py:27
  86.9 14.6 %collective-permute-start.17 = (bf16[128,1024]{1,0:T(8,128)(2,1)}, bf16[128,1024]{1,0:T(8,128)(2,1)S(1)}, u32[]{:S(2)}, u32[]{:S(2)}) collective-permute-start(bf16[128,1024]{1,0:T(8,128)(2,1)} %collective-permute-done.16), channel_id=1, source_target_pairs={{0,16},{16,0},{8,24},{24,8},{32,48},{48,32},{40,56},{56,40},{64,80... | collective-permute-start | bytes 786440 | tf_op jit(solution)/shard_map/ppermute | solution.py:27
  101.5 12.6 %collective-permute-start.18 = (bf16[128,1024]{1,0:T(8,128)(2,1)S(1)}, bf16[128,1024]{1,0:T(8,128)(2,1)S(1)}, u32[]{:S(2)}, u32[]{:S(2)}) collective-permute-start(bf16[128,1024]{1,0:T(8,128)(2,1)S(1)} %collective-permute-done.17), channel_id=1, source_target_pairs={{0,32},{32,0},{8,40},{40,8},{16,48},{48,16},{24,56},{56,24},{64,96... | collective-permute-start | bytes 786440 | tf_op jit(solution)/shard_map/ppermute | solution.py:27
  103.4 14.6 %collective-permute-start.2 = (bf16[128,1024]{1,0:T(8,128)(2,1)S(1)}, bf16[128,1024]{1,0:T(8,128)(2,1)S(1)}, u32[]{:S(2)}, u32[]{:S(2)}) collective-permute-start(bf16[128,1024]{1,0:T(8,128)(2,1)S(1)} %collective-permute-done.1), channel_id=1, source_target_pairs={{0,16},{16,0},{8,24},{24,8},{32,48},{48,32},{40,56},{56,40},{64,80... | collective-permute-start | bytes 786440 | tf_op jit(solution)/shard_map/ppermute | solution.py:27
  114.1 9.3 %collective-permute-start.19 = (bf16[128,1024]{1,0:T(8,128)(2,1)S(1)}, bf16[128,1024]{1,0:T(8,128)(2,1)S(1)}, u32[]{:S(2)}, u32[]{:S(2)}) collective-permute-start(bf16[128,1024]{1,0:T(8,128)(2,1)S(1)} %collective-permute-done.18), channel_id=1, source_target_pairs={{0,64},{64,0},{8,72},{72,8},{16,80},{80,16},{24,88},{88,24},{32,96... | collective-permute-start | bytes 786440 | tf_op jit(solution)/shard_map/ppermute | solution.py:27
  118.0 11.5 %collective-permute-start.3 = (bf16[128,1024]{1,0:T(8,128)(2,1)S(1)}, bf16[128,1024]{1,0:T(8,128)(2,1)S(1)}, u32[]{:S(2)}, u32[]{:S(2)}) collective-permute-start(bf16[128,1024]{1,0:T(8,128)(2,1)S(1)} %collective-permute-done.2), channel_id=1, source_target_pairs={{0,32},{32,0},{8,40},{40,8},{16,48},{48,16},{24,56},{56,24},{64,96... | collective-permute-start | bytes 786440 | tf_op jit(solution)/shard_map/ppermute | solution.py:27
  123.3 15.0 %collective-permute-start.20 = (bf16[128,1024]{1,0:T(8,128)(2,1)S(1)}, bf16[128,1024]{1,0:T(8,128)(2,1)S(1)}, u32[]{:S(2)}, u32[]{:S(2)}) collective-permute-start(bf16[128,1024]{1,0:T(8,128)(2,1)S(1)} %collective-permute-done.19), channel_id=1, source_target_pairs={{0,128},{128,0},{8,136},{136,8},{16,144},{144,16},{24,152},{152,24... | collective-permute-start | bytes 786440 | tf_op jit(solution)/shard_map/ppermute | solution.py:27
  129.5 52.7 %collective-permute-start.4 = (bf16[128,1024]{1,0:T(8,128)(2,1)S(1)}, bf16[128,1024]{1,0:T(8,128)(2,1)}, u32[]{:S(2)}, u32[]{:S(2)}) collective-permute-start(bf16[128,1024]{1,0:T(8,128)(2,1)S(1)} %collective-permute-done.3), channel_id=1, source_target_pairs={{0,64},{64,0},{8,72},{72,8},{16,80},{80,16},{24,88},{88,24},{32,96... | collective-permute-start | bytes 786440 | tf_op jit(solution)/shard_map/ppermute | solution.py:27
  138.4 48.7 %collective-permute-start.21 = (bf16[128,1024]{1,0:T(8,128)(2,1)S(1)}, bf16[128,1024]{1,0:T(8,128)(2,1)}, u32[]{:S(2)}, u32[]{:S(2)}) collective-permute-start(bf16[128,1024]{1,0:T(8,128)(2,1)S(1)} %collective-permute-done.20), channel_id=1, source_target_pairs={{0,256},{256,0},{8,264},{264,8},{16,272},{272,16},{24,280},{280,24... | collective-permute-start | bytes 786440 | tf_op jit(solution)/shard_map/ppermute | solution.py:27
  148.8 7.0 %collective-permute-start.25 = (bf16[128,8]{0,1:T(8,128)(2,1)S(1)}, bf16[128,8]{0,1:T(8,128)(2,1)S(1)}, u32[]{:S(2)}, u32[]{:S(2)}) collective-permute-start(bf16[128,8]{0,1:T(8,128)(2,1)S(1)} %collective-permute-done.24), channel_id=1, source_target_pairs={{0,32},{32,0},{8,40},{40,8},{16,48},{48,16},{24,56},{56,24},{64,96... | collective-permute-start | bytes 6152 | tf_op jit(solution)/shard_map/ppermute | solution.py:27
  167.8 9.6 %collective-permute-start.28 = (bf16[128,8]{0,1:T(8,128)(2,1)S(1)}, bf16[128,8]{0,1:T(8,128)(2,1)S(1)}, u32[]{:S(2)}, u32[]{:S(2)}) collective-permute-start(bf16[128,8]{0,1:T(8,128)(2,1)S(1)} %collective-permute-done.27), channel_id=1, source_target_pairs={{0,256},{256,0},{8,264},{264,8},{16,272},{272,16},{24,280},{280,24... | collective-permute-start | bytes 6152 | tf_op jit(solution)/shard_map/ppermute | solution.py:27
  175.5 142.3 %collective-permute-start.15 = (bf16[1,128,1024]{2,1,0:T(8,128)(2,1)}, bf16[1,128,1024]{2,1,0:T(8,128)(2,1)}, u32[]{:S(2)}, u32[]{:S(2)}) collective-permute-start(bf16[1,128,1024]{2,1,0:T(8,128)(2,1)} %param.9), channel_id=1, source_target_pairs={{8,0},{16,8},{24,16},{32,24},{40,32},{48,40},{56,48},{64,56},{72,6... | collective-permute-start | bytes 786440 | tf_op jit(solution)/shard_map/ppermute | solution.py:17
  177.4 18.1 %collective-permute-start.29 = (bf16[128,8]{0,1:T(8,128)(2,1)S(1)}, bf16[128,8]{0,1:T(8,128)(2,1)S(1)}, u32[]{:S(2)}, u32[]{:S(2)}) collective-permute-start(bf16[128,8]{0,1:T(8,128)(2,1)S(1)} %collective-permute-done.28), channel_id=1, source_target_pairs={{0,512},{512,0},{8,520},{520,8},{16,528},{528,16},{24,536},{536,24... | collective-permute-start | bytes 6152 | tf_op jit(solution)/shard_map/ppermute | solution.py:27
  182.3 17.5 %collective-permute-start.5 = (bf16[128,1024]{1,0:T(8,128)(2,1)}, bf16[128,1024]{1,0:T(8,128)(2,1)}, u32[]{:S(2)}, u32[]{:S(2)}) collective-permute-start(bf16[128,1024]{1,0:T(8,128)(2,1)} %collective-permute-done.4), channel_id=1, source_target_pairs={{0,128},{128,0},{8,136},{136,8},{16,144},{144,16},{24,152},{152,24... | collective-permute-start | bytes 786440 | tf_op jit(solution)/shard_map/ppermute | solution.py:27
  187.1 52.5 %collective-permute-start.22 = (bf16[128,1024]{1,0:T(8,128)(2,1)}, bf16[128,1024]{1,0:T(8,128)(2,1)S(1)}, u32[]{:S(2)}, u32[]{:S(2)}) collective-permute-start(bf16[128,1024]{1,0:T(8,128)(2,1)} %collective-permute-done.21), channel_id=1, source_target_pairs={{0,512},{512,0},{8,520},{520,8},{16,528},{528,16},{24,536},{536,24... | collective-permute-start | bytes 786440 | tf_op jit(solution)/shard_map/ppermute | solution.py:27
  199.8 112.4 %collective-permute-start.6 = (bf16[128,1024]{1,0:T(8,128)(2,1)}, bf16[128,1024]{1,0:T(8,128)(2,1)}, u32[]{:S(2)}, u32[]{:S(2)}) collective-permute-start(bf16[128,1024]{1,0:T(8,128)(2,1)} %collective-permute-done.5), channel_id=1, source_target_pairs={{0,256},{256,0},{8,264},{264,8},{16,272},{272,16},{24,280},{280,24... | collective-permute-start | bytes 786440 | tf_op jit(solution)/shard_map/ppermute | solution.py:27
  312.2 51.6 %collective-permute-start.7 = (bf16[128,1024]{1,0:T(8,128)(2,1)}, bf16[128,1024]{1,0:T(8,128)(2,1)S(1)}, u32[]{:S(2)}, u32[]{:S(2)}) collective-permute-start(bf16[128,1024]{1,0:T(8,128)(2,1)} %collective-permute-done.6), channel_id=1, source_target_pairs={{0,512},{512,0},{8,520},{520,8},{16,528},{528,16},{24,536},{536,24... | collective-permute-start | bytes 786440 | tf_op jit(solution)/shard_map/ppermute | solution.py:27
  (14 other events, 884.1 us)
Sparse Core Ops, SparseCore 0:
  312.3 163.4 reduce-scatter.1
where the time goes:
time: 484 us; the launch traced here: 483 us
  waiting for transfers between devices  265 us (55%)
  starting transfers between devices  123 us (25%)
  blocking collectives  69.4 us (14%)
  between operations  15.8 us (3%)
  other arithmetic  5.2 us (1%)
    ppermute x28, waiting for transfers between devices, swapped(): return lax.ppermute(block, axis, route)  152 us
    ppermute x28, starting transfers between devices, swapped(): return lax.ppermute(block, axis, route)  119 us
    reduce_scatter x1, waiting for transfers between devices, on_device(): lax.psum_scatter(jnp.dot(normed, weight, preferred_element_type=jnp.float...  110 us
    psum x1, blocking collectives, on_device(): forward_total = lax.psum(forward_local, 'tensor')  69.4 us
  transfers between devices with their start and end apart: 31, of which 22 were waited for; matrix products, arithmetic and copies ran while one was open for 2% of the time, Pallas kernels for 0%

commit v1 on v0

v1 whole, which is shorter than its diff:
```python
import functools

import jax
import jax.numpy as jnp
from jax import lax
from jax.experimental import pallas as pl
from jax.experimental.pallas import tpu as pltpu
from jax.sharding import PartitionSpec as P

MESH = pl.DeviceIdType.MESH
BLOCK = 128
ROW = 8
HALVES = 2
CHUNKS = 4

epsilon_norm = 1e-05
epsilon_scale = 1e-06

XS, GS, HELD, SCALE, XM = 0, 1, 2, 3, 4


def column_form(rows8):
    return jnp.concatenate([rows8] * 16, axis=0).T


def kernel(
    sizes,
    x_hbm, g_hbm, gain_hbm, w_hbm, kg_hbm, held_hbm, hs_hbm, flags_hbm,
    key_v, held_v, scale_v, grad_v,
    gain, w, kg, held, hs, flags,
    arr, down, rheld, rhs, xm,
    scaled, saved, yb, ss, kpf, kp, kss, ky, kys, kz_src, kzs_src, kz, kzs,
    sums, sy, sz_src, sz, sc_cols,
    lsem, send, recv, chain, token,
):
    sections, tensors, tok, feats, width = sizes
    ys, zlo = tensors // HALVES, sections // ROW
    zs = HALVES * zlo
    rt = tok // tensors
    nblk = feats // BLOCK
    crow = tok // CHUNKS
    f32 = jnp.float32

    s = lax.axis_index("section")
    t = lax.axis_index("tensor")
    r, lo = s % ROW, s // ROW
    hi, y = t // ys, t % ys
    z = hi * zlo + lo

    def at_z(step):
        there = (z + step + zs) % zs
        return ((there % zlo) * ROW + r, (there // zlo) * ys + y)

    def y_peer(k):
        return (s, hi * ys + (y + k) % ys)

    z_peer = (s, (1 - hi) * ys + y)
    nxt = ((s + 1) % sections, t)
    prv = ((s + sections - 1) % sections, t)
    mirror = (sections - 1 - s, t)
    mirror_x = ((2 * sections - 2 - s) % sections, t)
    own_x = mirror_x[0] == s

    locals_in = [
        pltpu.make_async_copy(a, b, lsem.at[i])
        for i, (a, b) in enumerate(
            ((w_hbm, w), (kg_hbm, kg), (gain_hbm, gain), (held_hbm, held), (hs_hbm, hs), (flags_hbm, flags))
        )
    ]
    for copy in locals_in:
        copy.start()

    def remote(number, src, dst, device):
        return pltpu.make_async_remote_copy(
            src_ref=src, dst_ref=dst, send_sem=send.at[number], recv_sem=recv.at[number],
            device_id=device, device_id_type=MESH,
        )

    x_copy = remote(XS, x_hbm, arr, nxt)
    g_copy = remote(GS, g_hbm, down, prv)
    h_copy = remote(HELD, held_hbm, rheld, mirror)
    hs_copy = remote(SCALE, hs_hbm, rhs, mirror)

    def x_rows(c):
        return x_hbm.at[pl.ds(c * crow, crow)], xm.at[pl.ds(c * crow, crow)]

    xm_copies = [remote(XM + c, *x_rows(c), mirror_x) for c in range(CHUNKS)]
    xm_own = [pltpu.make_async_copy(*x_rows(c), recv.at[XM + c]) for c in range(CHUNKS)]
    n = XM + CHUNKS
    ky_copies = [remote(n + k - 1, kp.at[(y + k) % ys], ky.at[k - 1], y_peer(k)) for k in range(1, ys)]
    n += ys - 1
    kys_copies = [remote(n + k - 1, kss.at[(y + k) % ys], kys.at[k - 1], y_peer(k)) for k in range(1, ys)]
    n += ys - 1
    kz_copy = remote(n, kz_src, kz, z_peer)
    kzs_copy = remote(n + 1, kzs_src, kzs, z_peer)
    n += 2
    sy_copies = [remote(n + k - 1, sums, sy.at[k - 1], y_peer(k)) for k in range(1, ys)]
    n += ys - 1
    sz_copy = remote(n, sz_src, sz, z_peer)

    def issue(stage):
        for copies, target in (((x_copy,), nxt), ((g_copy,), prv), ((hs_copy, h_copy), mirror)):
            apart = jnp.abs(target[0] // ROW - lo)
            first = jnp.where(apart > 0, 1, 0)
            for k in range(1, steps):
                first = jnp.where(apart >= 1 << k, k + 1, first)

            @pl.when(first == stage)
            def _():
                for copy in copies:
                    copy.start()

    steps = zlo.bit_length() - 1
    barrier = pltpu.get_barrier_semaphore()
    near = [(lo * ROW + (r + k) % ROW, t) for k in range(1, ROW)]
    near += [y_peer(k) for k in range(1, ys)] + [at_z(1), at_z(-1)]
    for device in near:
        pl.semaphore_signal(barrier, inc=1, device_id=device, device_id_type=MESH)
    pl.semaphore_wait(barrier, len(near))
    issue(0)
    for k in range(steps):
        for way in range(2):
            there = at_z((1 - 2 * way) << k)
            pl.semaphore_signal(chain.at[2 * k + way], inc=1, device_id=there, device_id_type=MESH)
        pl.semaphore_wait(chain.at[2 * k], 1)
        pl.semaphore_wait(chain.at[2 * k + 1], 1)
        issue(k + 1)

    for copy in locals_in:
        copy.wait()

    for c in range(0, feats, 256):
        cols = pl.ds(c, min(256, feats))
        part = lax.dot_general(
            kg[...], w[cols, :], (((1,), (1,)), ((), ())), preferred_element_type=f32
        )
        scaled[:, cols] = part * gain[:, cols]

    x_copy.wait_recv()
    total = jnp.zeros((tok, BLOCK), f32)
    for b in range(nblk):
        cols = pl.ds(b * BLOCK, BLOCK)
        v = arr[:, cols].astype(f32)
        total += v * v
        yb[:, cols] = (v * gain[:, cols]).astype(jnp.bfloat16)
    ss[...] = total
    for c in range(0, width, 256):
        cols = pl.ds(c, min(256, width))
        kpf[:, cols] = jnp.dot(yb[...], w[:, cols], preferred_element_type=f32)
    for yy in range(ys):
        for side in range(HALVES):
            half = hi if side == 0 else 1 - hi
            rows = pl.ds(pl.multiple_of((half * ys + yy) * rt, rt), rt)
            here = pl.ds(side * rt, rt)
            kp[yy, here, :] = kpf[rows, :].astype(jnp.bfloat16)
            kss[yy, here, :] = ss[rows, :]
    for copy in ky_copies + kys_copies:
        copy.start()
    for copy in ky_copies + kys_copies:
        copy.wait_recv()
    sides = []
    for side in range(HALVES):
        half = hi if side == 0 else 1 - hi
        rows = pl.ds(pl.multiple_of((half * ys + y) * rt, rt), rt)
        here = pl.ds(side * rt, rt)
        key_sum, sq_sum = kpf[rows, :], ss[rows, :]
        for k in range(ys - 1):
            key_sum = key_sum + ky[k, here, :].astype(f32)
            sq_sum = sq_sum + kys[k, here, :]
        sides.append((rows, key_sum, sq_sum))
    kz_src[...] = sides[1][1].astype(jnp.bfloat16)
    kzs_src[...] = sides[1][2]
    kz_copy.start()
    kzs_copy.start()
    own_rows = sides[0][0]
    kpf[own_rows, :] = sides[0][1]
    ss[own_rows, :] = sides[0][2]

    lane = lax.broadcasted_iota(jnp.int32, (2, sections), 1)
    mine = jnp.sum(jnp.where(lane == s, flags[...].astype(f32), 0.0), axis=1, keepdims=True)
    fetched, parked = mine[0:1, :], mine[1:2, :]

    hs_copy.wait_recv()
    h_copy.wait_recv()

    pick = jnp.broadcast_to(fetched, (tok, BLOCK)) > 0.5
    scales = column_form(jnp.where(jnp.broadcast_to(fetched, hs.shape) > 0.5, rhs[...], hs[...]))
    square = jnp.zeros((tok, BLOCK), f32)
    cross = jnp.zeros((tok, BLOCK), f32)
    for b in range(nblk):
        cols = pl.ds(b * BLOCK, BLOCK)
        v = jnp.where(pick, rheld[:, cols].astype(f32), held[:, cols].astype(f32))
        v = v * scales[:, b : b + 1]
        saved[:, cols] = v
        square += v * v
        cross += v * scaled[:, cols]
    lane = lax.broadcasted_iota(jnp.int32, (tok, BLOCK), 1)
    square = jnp.sum(square, axis=1, keepdims=True)
    cross = jnp.sum(cross, axis=1, keepdims=True)
    sums[...] = jnp.where(lane == 0, square, jnp.where(lane == 1, cross, 0.0)).T[:8, :]
    for copy in sy_copies:
        copy.start()
    for copy in sy_copies:
        copy.wait_recv()
    total = sums[...]
    for k in range(ys - 1):
        total = total + sy[k]
    sz_src[...] = total
    sz_copy.start()

    low = lo < zlo // 2

    @pl.when(jnp.logical_and(lo != zlo // 2 - 1, lo != zlo // 2))
    def _():
        pl.semaphore_wait(token, 1)

    @pl.when(jnp.logical_and(low, lo > 0))
    def _():
        pl.semaphore_signal(token, inc=1, device_id=at_z(-1), device_id_type=MESH)

    @pl.when(jnp.logical_and(jnp.logical_not(low), lo < zlo - 1))
    def _():
        pl.semaphore_signal(token, inc=1, device_id=at_z(1), device_id_type=MESH)

    @pl.when(own_x)
    def _():
        for copy in xm_own:
            copy.start()

    @pl.when(jnp.logical_not(own_x))
    def _():
        for copy in xm_copies:
            copy.start()

    kz_copy.wait_recv()
    kzs_copy.wait_recv()
    full = feats * tensors
    squares = jnp.sum(ss[own_rows, :] + kzs[...], axis=1, keepdims=True)
    inverse = lax.rsqrt(squares / full + epsilon_norm)
    key_v[...] = ((kpf[own_rows, :] + kz[...].astype(f32)) * inverse).astype(jnp.bfloat16)

    sz_copy.wait_recv()
    g_copy.wait_recv()
    totals = column_form(sz_src[...] + sz[...])
    inverse = lax.rsqrt(totals[:, 0:1] / full + epsilon_norm)
    factor = inverse * inverse * inverse * (totals[:, 1:2] / full)
    for b in range(nblk):
        cols = pl.ds(b * BLOCK, BLOCK)
        v = inverse * scaled[:, cols] - saved[:, cols] * factor
        grad_v[:, cols] = (down[:, cols].astype(f32) + v).astype(jnp.bfloat16)

    pick = jnp.broadcast_to(parked, (crow, BLOCK)) > 0.5
    lane = lax.broadcasted_iota(jnp.int32, (crow, BLOCK), 1)
    for c in range(CHUNKS):

        @pl.when(own_x)
        def _():
            xm_own[c].wait()

        @pl.when(jnp.logical_not(own_x))
        def _():
            xm_copies[c].wait_recv()

        rows = pl.ds(c * crow, crow)
        columns = jnp.zeros((crow, BLOCK), f32)
        for b in range(nblk):
            cols = pl.ds(b * BLOCK, BLOCK)
            v = jnp.where(pick, xm[rows, cols].astype(f32), arr[rows, cols].astype(f32))
            scale = jnp.max(jnp.abs(v), axis=1, keepdims=True) + epsilon_scale
            held_v[rows, cols] = (v / scale).astype(jnp.bfloat16)
            columns = jnp.where(lane == b, scale, columns)
        sc_cols[rows, :] = columns
    scale_v[...] = sc_cols[...].T[:8, :]

    for copy in [x_copy, g_copy, h_copy, hs_copy, kz_copy, kzs_copy, sz_copy] + ky_copies + kys_copies + sy_copies:
        copy.wait_send()

    @pl.when(jnp.logical_not(own_x))
    def _():
        for copy in xm_copies:
            copy.wait_send()


def flush(*refs):
    sources, targets, sem = refs[:4], refs[4:8], refs[8]
    copies = [pltpu.make_async_copy(a, b, sem.at[i]) for i, (a, b) in enumerate(zip(sources, targets))]
    for copy in copies:
        copy.start()
    for copy in copies:
        copy.wait()


def on_device(x_sent, grad_in, norm_gain, w_key, key_grad, held_in, held_scale, stash_flags):
    sections, tensors = lax.axis_size("section"), lax.axis_size("tensor")
    tok, feats = x_sent.shape[1:]
    width = w_key.shape[2]
    nblk = feats // BLOCK
    ys, zlo = tensors // HALVES, sections // ROW
    rt = tok // tensors
    bf16, f32 = jnp.bfloat16, jnp.float32
    v, dma = pltpu.VMEM, pltpu.SemaphoreType.DMA
    hs = held_scale[0].T
    copies = XM + CHUNKS + 3 * (ys - 1) + 3
    shapes = (((rt, width), bf16), ((tok, feats), bf16), ((nblk, tok), f32), ((tok, feats), bf16))
    here = pl.pallas_call(
        functools.partial(kernel, (sections, tensors, tok, feats, width)),
        out_shape=[v(*shape) for shape in shapes],
        in_specs=[pl.BlockSpec(memory_space=pltpu.HBM)] * 8,
        out_specs=[pl.BlockSpec(memory_space=v)] * 4,
        scratch_shapes=[
            v((1, feats), f32), v((feats, width), bf16), v((tok, width), bf16),
            v((tok, feats), bf16), v((nblk, tok), f32), v((2, sections), jnp.int32),
            v((tok, feats), bf16), v((tok, feats), bf16), v((tok, feats), bf16),
            v((nblk, tok), f32), v((tok, feats), bf16),
            v((tok, feats), f32), v((tok, feats), f32), v((tok, feats), bf16),
            v((tok, BLOCK), f32), v((tok, width), f32),
            v((ys, HALVES * rt, width), bf16), v((ys, HALVES * rt, BLOCK), f32),
            v((max(ys - 1, 1), HALVES * rt, width), bf16), v((max(ys - 1, 1), HALVES * rt, BLOCK), f32),
            v((rt, width), bf16), v((rt, BLOCK), f32), v((rt, width), bf16), v((rt, BLOCK), f32),
            v((8, tok), f32), v((max(ys - 1, 1), 8, tok), f32), v((8, tok), f32), v((8, tok), f32),
            v((tok, BLOCK), f32),
            dma((6,)), dma((copies,)), dma((copies,)),
            pltpu.SemaphoreType.REGULAR((2 * max(zlo.bit_length() - 1, 1),)), pltpu.SemaphoreType.REGULAR,
        ],
        compiler_params=pltpu.CompilerParams(
            collective_id=0, has_side_effects=True, vmem_limit_bytes=24 * 1024 * 1024
        ),
        name="tick",
    )(
        *(
            pltpu.with_memory_space_constraint(a, pltpu.HBM)
            for a in (x_sent[0], grad_in[0], norm_gain, w_key[0], key_grad[0], held_in[0], hs, stash_flags.T)
        )
    )
    key, held, scale, grad = pl.pallas_call(
        flush,
        out_shape=[jax.ShapeDtypeStruct(*shape) for shape in shapes],
        in_specs=[pl.BlockSpec(memory_space=v)] * 4,
        out_specs=[pl.BlockSpec(memory_space=pl.ANY)] * 4,
        scratch_shapes=[dma((4,))],
        compiler_params=pltpu.CompilerParams(vmem_limit_bytes=8 * 1024 * 1024),
        name="flush",
    )(*here)
    return key[None], held[None], scale.T[None], grad[None]


def solution(mesh):
    return jax.shard_map(
        on_device,
        mesh=mesh,
        in_specs=(
            P("section", None, "tensor"),
            P("section", None, "tensor"),
            P("section", "tensor"),
            P("section", "tensor", None),
            P("section", None, None),
            P("section", None, "tensor"),
            P("section", None, "tensor"),
            P(),
        ),
        out_specs=(
            P("section", "tensor", None),
            P("section", None, "tensor"),
            P("section", None, "tensor"),
            P("section", None, "tensor"),
        ),
        check_vma=False,
    )
```

time: 484 us -> 121 us (0.25)
  the two profiles are of different devices: /device:TPU:2 before, /device:TPU:230 now
where the time goes in v1:
time: 121 us
  Pallas kernels  121 us (100%)
    pallas_call x1, Pallas kernels, on_device(): pl.pallas_call(functools.partial(kernel, (sections, tensors, tok, feats,...  120 us

profile of v1, /device:TPU:230, one launch (start us, length us, event | category | flops | bytes accessed | tf_op | source)
XLA Modules:
  0.0 121.3 jit_solution(8163232121818740579)
XLA Ops:
  0.6 119.8 %tick.1 = (bf16[16,1024]{1,0:T(8,128)(2,1)S(1)}, bf16[128,1024]{1,0:T(8,128)(2,1)S(1)}, f32[8,128]{1,0:T(8,128)S(1)}, bf16[128,1024]{1,0:T(8,128)(2,1)S(1)}) custom-call(bf16[128,1024]{1,0:T(8,128)(2,1)} %bitcast.16, bf16[128,1024]{1,0:T(8,128)(2,1)} %bitcast.17, f32[1,1024]{1,0:T(1,128)} %gain_hbm.1, bf16[1024,1024]{1,0:T(8,128)(2,1)} %bitcast.15, ...), custom_call_target="tpu_custom_call" | custom-call | tf_op jit(solution)/shard_map/tick/pallas_call | solution.py:305
  120.4 0.8 flush.1

commit v2 on v1

--- a/solution.py
+++ b/solution.py
@@ -12,6 +12,7 @@
 ROW = 8
 HALVES = 2
 CHUNKS = 4
+FRONT = 1
 
 epsilon_norm = 1e-05
 epsilon_scale = 1e-06
@@ -31,7 +32,7 @@
     arr, down, rheld, rhs, xm,
     scaled, saved, yb, ss, kpf, kp, kss, ky, kys, kz_src, kzs_src, kz, kzs,
     sums, sy, sz_src, sz, sc_cols,
-    lsem, send, recv, chain, token,
+    lsem, send, recv, chain, token, hello,
 ):
     sections, tensors, tok, feats, width = sizes
     ys, zlo = tensors // HALVES, sections // ROW
@@ -98,33 +99,66 @@
     n += ys - 1
     sz_copy = remote(n, sz_src, sz, z_peer)
 
-    def issue(stage):
-        for copies, target in (((x_copy,), nxt), ((g_copy,), prv), ((hs_copy, h_copy), mirror)):
-            apart = jnp.abs(target[0] // ROW - lo)
-            first = jnp.where(apart > 0, 1, 0)
-            for k in range(1, steps):
-                first = jnp.where(apart >= 1 << k, k + 1, first)
-
-            @pl.when(first == stage)
-            def _():
-                for copy in copies:
-                    copy.start()
-
-    steps = zlo.bit_length() - 1
+    low = lo < zlo // 2
+    inner = jnp.where(low, zlo // 2 - 1 - lo, lo - zlo // 2)
+
+    @pl.when(own_x)
+    def _():
+        for copy in xm_own:
+            copy.start()
+
     barrier = pltpu.get_barrier_semaphore()
+    last = ROW - 1
     near = [(lo * ROW + (r + k) % ROW, t) for k in range(1, ROW)]
     near += [y_peer(k) for k in range(1, ys)] + [at_z(1), at_z(-1)]
-    for device in near:
+    mirror_row = (zlo - 1 - lo) * ROW
+    greet = jnp.where(r == 0, last - 1, jnp.where(r == last, 1, last - r))
+    for device in near + [(mirror_row + greet, t)]:
         pl.semaphore_signal(barrier, inc=1, device_id=device, device_id_type=MESH)
-    pl.semaphore_wait(barrier, len(near))
-    issue(0)
-    for k in range(steps):
-        for way in range(2):
-            there = at_z((1 - 2 * way) << k)
-            pl.semaphore_signal(chain.at[2 * k + way], inc=1, device_id=there, device_id_type=MESH)
-        pl.semaphore_wait(chain.at[2 * k], 1)
-        pl.semaphore_wait(chain.at[2 * k + 1], 1)
-        issue(k + 1)
+    first, final = s == 0, s == sections - 1
+    to_next = jnp.logical_and(r == last, jnp.logical_not(final))
+    to_prev = jnp.logical_and(r == 0, jnp.logical_not(first))
+    for crosses, device in ((to_next, nxt), (to_prev, prv)):
+
+        @pl.when(crosses)
+        def _():
+            pl.semaphore_signal(barrier, inc=1, device_id=device, device_id_type=MESH)
+
+    edge = jnp.logical_or(r == 0, r == last)
+    expected = jnp.where(edge, 0, 1) + jnp.where(r == 1, 1, 0) + jnp.where(r == last - 1, 1, 0)
+    expected = expected + jnp.where(to_next, 1, 0) + jnp.where(to_prev, 1, 0)
+    pl.semaphore_wait(barrier, len(near) + expected)
+
+    @pl.when(jnp.logical_not(final))
+    def _():
+        x_copy.start()
+
+    @pl.when(jnp.logical_not(first))
+    def _():
+        g_copy.start()
+
+    @pl.when(r == 1)
+    def _():
+        pl.semaphore_signal(hello, inc=1, device_id=(lo * ROW, t), device_id_type=MESH)
+
+    @pl.when(r == last - 1)
+    def _():
+        pl.semaphore_signal(hello, inc=1, device_id=(lo * ROW + last, t), device_id_type=MESH)
+
+    @pl.when(edge)
+    def _():
+        pl.semaphore_wait(hello, 1)
+
+    @pl.when(final)
+    def _():
+        x_copy.start()
+
+    hs_copy.start()
+    h_copy.start()
+
+    @pl.when(first)
+    def _():
+        g_copy.start()
 
     for copy in locals_in:
         copy.wait()
@@ -135,6 +169,13 @@
             kg[...], w[cols, :], (((1,), (1,)), ((), ())), preferred_element_type=f32
         )
         scaled[:, cols] = part * gain[:, cols]
+
+    for k in range(zlo.bit_length() - 1):
+        for way in range(2):
+            there = at_z((1 - 2 * way) << k)
+            pl.semaphore_signal(chain.at[2 * k + way], inc=1, device_id=there, device_id_type=MESH)
+        pl.semaphore_wait(chain.at[2 * k], 1)
+        pl.semaphore_wait(chain.at[2 * k + 1], 1)
 
     x_copy.wait_recv()
     total = jnp.zeros((tok, BLOCK), f32)
@@ -183,6 +224,11 @@
     hs_copy.wait_recv()
     h_copy.wait_recv()
 
+    @pl.when(jnp.logical_and(inner < FRONT, jnp.logical_not(own_x)))
+    def _():
+        for copy in xm_copies:
+            copy.start()
+
     pick = jnp.broadcast_to(fetched, (tok, BLOCK)) > 0.5
     scales = column_form(jnp.where(jnp.broadcast_to(fetched, hs.shape) > 0.5, rhs[...], hs[...]))
     square = jnp.zeros((tok, BLOCK), f32)
@@ -208,26 +254,21 @@
     sz_src[...] = total
     sz_copy.start()
 
-    low = lo < zlo // 2
-
-    @pl.when(jnp.logical_and(lo != zlo // 2 - 1, lo != zlo // 2))
+    @pl.when(inner > 0)
     def _():
         pl.semaphore_wait(token, 1)
 
-    @pl.when(jnp.logical_and(low, lo > 0))
+    outward = inner < zlo // 2 - 1
+
+    @pl.when(jnp.logical_and(outward, low))
     def _():
         pl.semaphore_signal(token, inc=1, device_id=at_z(-1), device_id_type=MESH)
 
-    @pl.when(jnp.logical_and(jnp.logical_not(low), lo < zlo - 1))
+    @pl.when(jnp.logical_and(outward, jnp.logical_not(low)))
     def _():
         pl.semaphore_signal(token, inc=1, device_id=at_z(1), device_id_type=MESH)
 
-    @pl.when(own_x)
-    def _():
-        for copy in xm_own:
-            copy.start()
-
-    @pl.when(jnp.logical_not(own_x))
+    @pl.when(jnp.logical_and(inner >= FRONT, jnp.logical_not(own_x)))
     def _():
         for copy in xm_copies:
             copy.start()
@@ -320,7 +361,7 @@
             v((8, tok), f32), v((max(ys - 1, 1), 8, tok), f32), v((8, tok), f32), v((8, tok), f32),
             v((tok, BLOCK), f32),
             dma((6,)), dma((copies,)), dma((copies,)),
-            pltpu.SemaphoreType.REGULAR((2 * max(zlo.bit_length() - 1, 1),)), pltpu.SemaphoreType.REGULAR,
+            pltpu.SemaphoreType.REGULAR((2 * max(zlo.bit_length() - 1, 1),)), pltpu.SemaphoreType.REGULAR, pltpu.SemaphoreType.REGULAR,
         ],
         compiler_params=pltpu.CompilerParams(
             collective_id=0, has_side_effects=True, vmem_limit_bytes=24 * 1024 * 1024

time: 121 us -> 116 us (0.959)
  the two profiles are of different devices: /device:TPU:230 before, /device:TPU:774 now
where the time goes in v2:
time: 116 us
  Pallas kernels  115 us (99%)
    pallas_call x1, Pallas kernels, on_device(): pl.pallas_call(functools.partial(kernel, (sections, tensors, tok, feats,...  114 us

profile of v2, /device:TPU:774, one launch (start us, length us, event | category | flops | bytes accessed | tf_op | source)
XLA Modules:
  0.0 115.8 jit_solution(9369976984220962047)
XLA Ops:
  0.6 114.3 %tick.1 = (bf16[16,1024]{1,0:T(8,128)(2,1)S(1)}, bf16[128,1024]{1,0:T(8,128)(2,1)S(1)}, f32[8,128]{1,0:T(8,128)S(1)}, bf16[128,1024]{1,0:T(8,128)(2,1)S(1)}) custom-call(bf16[128,1024]{1,0:T(8,128)(2,1)} %bitcast.16, bf16[128,1024]{1,0:T(8,128)(2,1)} %bitcast.17, f32[1,1024]{1,0:T(1,128)} %gain_hbm.1, bf16[1024,1024]{1,0:T(8,128)(2,1)} %bitcast.15, ...), custom_call_target="tpu_custom_call" | custom-call | tf_op jit(solution)/shard_map/tick/pallas_call | solution.py:346
  115.0 0.8 flush.1

commit v3 on v2

--- a/solution.py
+++ b/solution.py
@@ -210,7 +210,9 @@
             sq_sum = sq_sum + kys[k, here, :]
         sides.append((rows, key_sum, sq_sum))
     kz_src[...] = sides[1][1].astype(jnp.bfloat16)
-    kzs_src[...] = sides[1][2]
+    squares = jnp.sum(sides[1][2], axis=1, keepdims=True)
+    squares = jnp.broadcast_to(squares, (rt, BLOCK))
+    kzs_src[...] = jnp.concatenate([squares] * (BLOCK // rt), axis=0).T[0:1, :]
     kz_copy.start()
     kzs_copy.start()
     own_rows = sides[0][0]
@@ -276,7 +278,8 @@
     kz_copy.wait_recv()
     kzs_copy.wait_recv()
     full = feats * tensors
-    squares = jnp.sum(ss[own_rows, :] + kzs[...], axis=1, keepdims=True)
+    squares = jnp.sum(ss[own_rows, :], axis=1, keepdims=True)
+    squares = squares + jnp.broadcast_to(kzs[...], (BLOCK, BLOCK)).T[:rt, 0:1]
     inverse = lax.rsqrt(squares / full + epsilon_norm)
     key_v[...] = ((kpf[own_rows, :] + kz[...].astype(f32)) * inverse).astype(jnp.bfloat16)
 
@@ -357,7 +360,7 @@
             v((tok, BLOCK), f32), v((tok, width), f32),
             v((ys, HALVES * rt, width), bf16), v((ys, HALVES * rt, BLOCK), f32),
             v((max(ys - 1, 1), HALVES * rt, width), bf16), v((max(ys - 1, 1), HALVES * rt, BLOCK), f32),
-            v((rt, width), bf16), v((rt, BLOCK), f32), v((rt, width), bf16), v((rt, BLOCK), f32),
+            v((rt, width), bf16), v((1, BLOCK), f32), v((rt, width), bf16), v((1, BLOCK), f32),
             v((8, tok), f32), v((max(ys - 1, 1), 8, tok), f32), v((8, tok), f32), v((8, tok), f32),
             v((tok, BLOCK), f32),
             dma((6,)), dma((copies,)), dma((copies,)),

time: 116 us -> 115 us (level)
    pallas_call x1, Pallas kernels: 114 us -> 113 us  [on_device(): pl.pallas_call(functools.partial(kernel, (sections, tensors, tok, feats,...]
where the time goes in v3:
time: 115 us; the launch traced here: 114 us
  Pallas kernels  114 us (99%)
    pallas_call x1, Pallas kernels, on_device(): pl.pallas_call(functools.partial(kernel, (sections, tensors, tok, feats,...  113 us

profile of v3, /device:TPU:774, one launch (start us, length us, event | category | flops | bytes accessed | tf_op | source)
XLA Modules:
  0.0 114.4 jit_solution(5915732141420428490)
XLA Ops:
  0.6 112.9 %tick.1 = (bf16[16,1024]{1,0:T(8,128)(2,1)S(1)}, bf16[128,1024]{1,0:T(8,128)(2,1)S(1)}, f32[8,128]{1,0:T(8,128)S(1)}, bf16[128,1024]{1,0:T(8,128)(2,1)S(1)}) custom-call(bf16[128,1024]{1,0:T(8,128)(2,1)} %bitcast.16, bf16[128,1024]{1,0:T(8,128)(2,1)} %bitcast.17, f32[1,1024]{1,0:T(1,128)} %gain_hbm.1, bf16[1024,1024]{1,0:T(8,128)(2,1)} %bitcast.15, ...), custom_call_target="tpu_custom_call" | custom-call | tf_op jit(solution)/shard_map/tick/pallas_call | solution.py:349
  113.6 0.8 flush.1
